TPU v7x, 32 devices: a whole 2x2x4 slice. The times are simulated.
32 devices in a mesh: freq: 2 (over x), row: 16 (over z, y, core).
Axes of the slice: x: 2, y: 2, z: 4, core: 2. Of those that a mesh axis runs over, the one named last changes fastest.
Arguments:
- data_real: bfloat16 [16384, 8192], P(('freq', 'row')), parts along dimension 0, may hold values from -6 to 6
- data_imag: bfloat16 [16384, 8192], P(('freq', 'row')), parts along dimension 0, may hold values from -6 to 6
- counts: int32 [8, 8], replicated, may hold values from 0 to 4
- source_cols: int32 [128], replicated, may hold values from 0 to 8191, as said below
Outputs:
- pred_real: float32 [16384, 128], P(('freq', 'row')), parts along dimension 0
- pred_imag: float32 [16384, 128], P(('freq', 'row')), parts along dimension 0
There are 2 independent parts, one for each index of `freq`. A program takes and returns all parts, laid end to end along the dimension named above; an argument that names none is the same for every part. Nothing has to cross between parts.
Inputs may be any that keep to these rules, and one draw needn't show every extreme that they name: `source_cols`: 128 distinct grid points; 0 and 8191 are always among them.
All inputs are finite; a program needn't handle non-finite values.
Results may differ from a plain program's by a relative error of at most 0.0029.
Values may be sent and summed in bfloat16 or wider, within the bound.
A program may use at most 128 MiB of HBM per device.

v0:
```python
import math
import jax
import jax.numpy as jnp
from jax import lax
from jax.sharding import PartitionSpec as P

TILES = 8


def tile_weights(counts, row_ids, width):
    tile = width // TILES
    onehot = (row_ids[:, None] // tile == jnp.arange(TILES, dtype=jnp.int32)[None, :]).astype(
        jnp.float32
    )
    table = counts.astype(jnp.float32)
    forward = jnp.dot(onehot, table, precision=lax.Precision.HIGHEST)
    backward = jnp.dot(onehot, table.T, precision=lax.Precision.HIGHEST)
    height = row_ids.shape[0]
    forward = jnp.broadcast_to(forward[:, :, None], (height, TILES, tile)).reshape(height, width)
    backward = jnp.broadcast_to(backward[:, :, None], (height, TILES, tile)).reshape(height, width)
    return (forward, backward)


def complex_pair(left_real, left_imag, right_real, right_imag, dims):
    dot_rr = lax.dot_general(left_real, right_real, dims, preferred_element_type=jnp.float32)
    dot_ii = lax.dot_general(left_imag, right_imag, dims, preferred_element_type=jnp.float32)
    dot_ri = lax.dot_general(left_real, right_imag, dims, preferred_element_type=jnp.float32)
    dot_ir = lax.dot_general(left_imag, right_real, dims, preferred_element_type=jnp.float32)
    return jnp.concatenate([dot_rr - dot_ii, dot_ri + dot_ir], axis=1)


def shards(data_real, data_imag, counts, source_cols):
    rows, width = data_real.shape
    mirror_real, mirror_imag = (
        lax.all_to_all(data_real, "row", split_axis=1, concat_axis=0, tiled=True),
        lax.all_to_all(data_imag, "row", split_axis=1, concat_axis=0, tiled=True),
    )
    row_ids = lax.axis_index("row") * rows + jnp.arange(rows, dtype=jnp.int32)
    forward, backward = tile_weights(counts, row_ids, width)
    denom = jnp.maximum(forward + backward, 1.0)
    sym_real = (
        (forward * data_real.astype(jnp.float32) + backward * mirror_real.T.astype(jnp.float32))
        / denom
    ).astype(jnp.bfloat16)
    sym_imag = (
        (forward * data_imag.astype(jnp.float32) + backward * mirror_imag.T.astype(jnp.float32))
        / denom
    ).astype(jnp.bfloat16)
    panel_real = jnp.take(sym_real, source_cols, axis=1)
    panel_imag = jnp.take(sym_imag, source_cols, axis=1)
    sources = source_cols.shape[0]
    factor = -1.0 / math.sqrt(width)
    piece_real = lax.all_gather(panel_real, "row", axis=0, tiled=True)
    piece_imag = lax.all_gather(panel_imag, "row", axis=0, tiled=True)
    summed = complex_pair(sym_real, sym_imag, piece_real, piece_imag, (((1,), (0,)), ((), ())))
    predicted = factor * summed
    return (predicted[:, :sources], predicted[:, sources:])


def solution(mesh):
    placed = (P(("freq", "row"), None), P(("freq", "row"), None), P(), P())
    return jax.shard_map(
        shards,
        mesh=mesh,
        in_specs=placed,
        out_specs=(P(("freq", "row"), None), P(("freq", "row"), None)),
        check_vma=False,
    )
```

profile of v0, /device:TPU:0, one launch (start us, length us, event | category | flops | bytes accessed | tf_op | source)
XLA Modules:
  0.0 530.0 jit_solution(13418963480100498488)
XLA Ops:
  7.2 7.5 %copy.17 = bf16[64,16,8,512]{3,2,0,1:T(8,128)(2,1)} copy(bf16[64,16,8,512]{3,2,1,0:T(8,128)(2,1)} %bitcast.68) | data formatting | bytes 16777216 | tf_op jit(solution)/shard_map/all_to_all | solution.py:35
  14.7 7.4 %all-to-all-start = ((bf16[512,16,512]{2,0,1:T(8,128)(2,1)}), bf16[512,16,512]{2,0,1:T(8,128)(2,1)}, u32[]{:S(2)}, u32[]{:S(2)}) async-start(bf16[512,16,512]{2,0,1:T(8,128)(2,1)} %bitcast.71), calls=%async_computation | async-start | bytes 16777216 | tf_op jit(solution)/shard_map/all_to_all | solution.py:35
  22.1 7.5 %copy.16 = bf16[64,16,8,512]{3,2,0,1:T(8,128)(2,1)} copy(bf16[64,16,8,512]{3,2,1,0:T(8,128)(2,1)} %bitcast.69) | data formatting | bytes 16777216 | tf_op jit(solution)/shard_map/all_to_all | solution.py:36
  29.7 143.2 %all-to-all-done = bf16[512,16,512]{2,0,1:T(8,128)(2,1)} async-done(((bf16[512,16,512]{2,0,1:T(8,128)(2,1)}), bf16[512,16,512]{2,0,1:T(8,128)(2,1)}, u32[]{:S(2)}, u32[]{:S(2)}) %all-to-all-start) | async-done | bytes 8388640 | tf_op jit(solution)/shard_map/all_to_all | solution.py:35
  172.8 36.5 %all-to-all-start.1 = ((bf16[512,16,512]{2,0,1:T(8,128)(2,1)}), bf16[512,16,512]{2,0,1:T(8,128)(2,1)}, u32[]{:S(2)}, u32[]{:S(2)}) async-start(bf16[512,16,512]{2,0,1:T(8,128)(2,1)} %bitcast.70), calls=%async_computation.1 | async-start | bytes 16777216 | tf_op jit(solution)/shard_map/all_to_all | solution.py:36
  209.4 0.0 all-gather.3.cloned.1.call-start
  209.5 12.0 %copy.6 = bf16[512,8192]{0,1:T(8,128)(2,1)} copy(bf16[512,8192]{1,0:T(8,128)(2,1)} %param.6) | data formatting | bytes 16777216 | tf_op args[0]
  221.4 0.0 copy-start.3
  221.5 0.0 copy-start.2
  221.5 11.5 %copy.8 = bf16[512,8192]{0,1:T(8,128)(2,1)} copy(bf16[512,8192]{1,0:T(8,128)(2,1)} %param.7) | data formatting | bytes 16777216 | tf_op args[1]
  233.0 0.0 copy-done.3
  233.0 0.0 copy-done.2
  233.0 0.3 fusion.7
  233.3 0.3 fusion.8
  233.7 126.5 %all-to-all-done.1 = bf16[512,16,512]{2,0,1:T(8,128)(2,1)} async-done(((bf16[512,16,512]{2,0,1:T(8,128)(2,1)}), bf16[512,16,512]{2,0,1:T(8,128)(2,1)}, u32[]{:S(2)}, u32[]{:S(2)}) %all-to-all-start.1) | async-done | bytes 8388640 | tf_op jit(solution)/shard_map/all_to_all | solution.py:36
  360.1 18.6 %fusion.2 = (bf16[512,8192]{0,1:T(8,128)(2,1)}, bf16[512,8192]{0,1:T(8,128)(2,1)}) fusion(bf16[512,8192]{0,1:T(8,128)(2,1)} %copy.6, f32[512,8]{0,1:T(8,128)S(1)} %fusion.7, f32[512,8]{0,1:T(8,128)S(1)} %fusion.8, bf16[512,16,512]{2,0,1:T(8,128)(2,1)} %all-to-all-done, bf16[512,16,512]{2,0,1:T(8,128)(2,1)} %all-to-all-done.1, bf16[512,8192]{0,1:T(8,128)(2,1)} %copy.8), kind=kLoop, calls=%fused_computation.9 | loop fusion | flops 67108864 | bytes 50364416 | tf_op jit(solution)/shard_map/convert_element_type | solution.py:44
  378.7 5.3 %gather_fusion = bf16[128,512]{1,0:T(8,128)(2,1)S(1)} fusion(bf16[512,8192]{0,1:T(8,128)(2,1)} %get-tuple-element.7, s32[1024]{0:T(1024)S(1)} %pad_clamp_fusion), kind=kCustom, calls=%fused_computation.clone | custom fusion | bytes 262656 | tf_op jit(solution)/shard_map/jit(_take)/gather | solution.py:49
  384.0 5.3 %gather_fusion.1 = bf16[128,512]{1,0:T(8,128)(2,1)S(1)} fusion(bf16[512,8192]{0,1:T(8,128)(2,1)} %get-tuple-element.8, s32[1024]{0:T(1024)S(1)} %pad_clamp_fusion), kind=kCustom, calls=%fused_computation.1.clone | custom fusion | bytes 262656 | tf_op jit(solution)/shard_map/jit(_take)/gather | solution.py:50
  389.3 0.8 select_bitcast_fusion.1
  390.1 0.0 all-gather.3.cloned.1.call-update
  390.2 0.2 all-gather.5.cloned.1.call-start
  390.4 0.5 all-gather.5.cloned.1.call-update
  390.9 72.4 %all-gather.3.cloned.1.call-done = bf16[8192,128]{0,1:T(8,128)(2,1)} async-done(((bf16[512,128]{0,1:T(8,128)(2,1)}), bf16[8192,128]{0,1:T(8,128)(2,1)}) %all-gather.3.cloned.1.call-update) | async-done | bytes 2097168 | tf_op jit(solution)/shard_map/all_gather | solution.py:53
  463.3 5.3 fusion.17
  468.6 37.6 %all-gather.5.cloned.1.call-done = bf16[8192,128]{0,1:T(8,128)(2,1)} async-done(((bf16[512,128]{0,1:T(8,128)(2,1)}), bf16[8192,128]{0,1:T(8,128)(2,1)}) %all-gather.5.cloned.1.call-update) | async-done | bytes 2097168 | tf_op jit(solution)/shard_map/all_gather | solution.py:54
  506.2 0.0 copy-start.1
  506.2 5.4 %fusion.18 = f32[512,128]{0,1:T(8,128)S(1)} fusion(bf16[8192,128]{0,1:T(8,128)(2,1)} %all-gather.5.cloned.1.call-done, bf16[512,8192]{0,1:T(8,128)(2,1)} %get-tuple-element.7), kind=kOutput, calls=%fused_computation.42 | convolution fusion | flops 1073741824 | bytes 10747904 | tf_op jit(solution)/shard_map/dot_general | solution.py:27
  511.6 0.0 copy-done.1
  511.6 0.0 copy-start
  511.6 4.9 convolution_subtract_fusion
  516.6 0.0 copy-done
  516.6 4.8 convolution_add_fusion
  521.3 0.1 maximum_multiply_fusion
  521.5 0.8 copy.10
  522.3 0.8 copy.11
  (5 shorter events, 0.1 us)
Async XLA Ops:
  14.7 158.2 %all-to-all-start = ((bf16[512,16,512]{2,0,1:T(8,128)(2,1)}), bf16[512,16,512]{2,0,1:T(8,128)(2,1)}, u32[]{:S(2)}, u32[]{:S(2)}) async-start(bf16[512,16,512]{2,0,1:T(8,128)(2,1)} %bitcast.71), calls=%async_computation | async-start | bytes 16777216 | tf_op jit(solution)/shard_map/all_to_all | solution.py:35
  172.8 187.3 %all-to-all-start.1 = ((bf16[512,16,512]{2,0,1:T(8,128)(2,1)}), bf16[512,16,512]{2,0,1:T(8,128)(2,1)}, u32[]{:S(2)}, u32[]{:S(2)}) async-start(bf16[512,16,512]{2,0,1:T(8,128)(2,1)} %bitcast.70), calls=%async_computation.1 | async-start | bytes 16777216 | tf_op jit(solution)/shard_map/all_to_all | solution.py:36
  209.4 253.9 %all-gather.3.cloned.1.call-start = ((), (), s32[]{:S(2)}) async-start(), calls=%async_computation.2 | async-start | bytes 2228224 | tf_op jit(solution)/shard_map/all_gather | solution.py:53
  221.4 11.5 %copy-start.3 = (s32[128]{0:T(128)S(1)}, s32[128]{0:T(128)}, u32[]{:S(2)}) copy-start(s32[128]{0:T(128)} %param.9) | copy-start | bytes 1540
  221.5 11.6 %copy-start.2 = (s32[8,8]{1,0:T(8,128)S(1)}, s32[8,8]{1,0:T(8,128)}, u32[]{:S(2)}) copy-start(s32[8,8]{1,0:T(8,128)} %param.8) | copy-start | bytes 772
  390.2 116.0 %all-gather.5.cloned.1.call-start = ((), (), s32[]{:S(2)}) async-start(), calls=%async_computation.3 | async-start | bytes 2228224 | tf_op jit(solution)/shard_map/all_gather | solution.py:54
  506.2 5.4 %copy-start.1 = (bf16[8192,128]{0,1:T(8,128)(2,1)S(1)}, bf16[8192,128]{0,1:T(8,128)(2,1)}, u32[]{:S(2)}) copy-start(bf16[8192,128]{0,1:T(8,128)(2,1)} %all-gather.5.cloned.1.call-done) | copy-start | bytes 6291460
  511.6 4.9 copy-start
Sparse Core Ops, SparseCore 0:
  390.3 72.9 all-gather.2
  466.0 40.1 all-gather.4
where the time goes:
time: 531 us; the launch traced here: 530 us
  waiting for transfers between devices  380 us (72%)
  local copies, waits for them, and re-layouts  50.9 us (10%)
  starting transfers between devices  44.2 us (8%)
  matrix products  21 us (4%)
  other arithmetic  19.4 us (4%)
  between operations  14.2 us (3%)
    all_to_all x1, waiting for transfers between devices, shards(): lax.all_to_all(data_real, 'row', split_axis=1, concat_axis=0, tiled=True)  143 us
    all_to_all x1, waiting for transfers between devices, shards(): lax.all_to_all(data_imag, 'row', split_axis=1, concat_axis=0, tiled=True)  126 us
    all_gather x1, waiting for transfers between devices, shards(): piece_real = lax.all_gather(panel_real, 'row', axis=0, tiled=True)  72.4 us
    all_gather x1, waiting for transfers between devices, shards(): piece_imag = lax.all_gather(panel_imag, 'row', axis=0, tiled=True)  37.6 us
    all_to_all x1, starting transfers between devices, shards(): lax.all_to_all(data_imag, 'row', split_axis=1, concat_axis=0, tiled=True)  36.5 us
    unnamed x12, local copies, waits for them, and re-layouts  25.2 us
    convert_element_type x1, other arithmetic, shards(): sym_real = ((forward * data_real.astype(jnp.float32) + backward * mirror_...  18.6 us
  transfers between devices with their start and end apart: 4, of which 4 were waited for; matrix products, arithmetic and copies ran while one was open for 7% of the time, Pallas kernels for 0%

commit v1 on v0

--- a/solution.py
+++ b/solution.py
@@ -5,6 +5,17 @@
 from jax.sharding import PartitionSpec as P
 
 TILES = 8
+
+
+def gather_by_hops(x, mesh_axis, d):
+    count = lax.axis_size(mesh_axis)
+    right = [(i, (i + 1) % count) for i in range(count)]
+    blocks = [x]
+    for stride in range(1, count):
+        blocks = [lax.ppermute(blocks[0], mesh_axis, right), *blocks]
+    whole = jnp.concatenate(blocks, axis=d)
+    shift = (lax.axis_index(mesh_axis) + 1) * blocks[-1].shape[d]
+    return jnp.roll(whole, shift, axis=d)
 
 
 def tile_weights(counts, row_ids, width):
@@ -51,7 +62,7 @@
     sources = source_cols.shape[0]
     factor = -1.0 / math.sqrt(width)
     piece_real = lax.all_gather(panel_real, "row", axis=0, tiled=True)
-    piece_imag = lax.all_gather(panel_imag, "row", axis=0, tiled=True)
+    piece_imag = gather_by_hops(panel_imag, "row", 0)
     summed = complex_pair(sym_real, sym_imag, piece_real, piece_imag, (((1,), (0,)), ((), ())))
     predicted = factor * summed
     return (predicted[:, :sources], predicted[:, sources:])

time: 531 us -> 585 us (1.10)
  waiting for transfers between devices: 380 us -> 413 us
  local copies, waits for them, and re-layouts: 50.9 us -> 73.1 us
    ppermute x0 -> x15, waiting for transfers between devices: none -> 136 us  [gather_by_hops(): blocks = [lax.ppermute(blocks[0], mesh_axis, right), *blocks]]
    all_gather x1, waiting for transfers between devices: 72.4 us -> 7.65 us  [shards(): piece_real = lax.all_gather(panel_real, 'row', axis=0, tiled=True)]
    all_gather x1 -> x0, waiting for transfers between devices: 37.6 us -> none  [shards(): piece_imag = lax.all_gather(panel_imag, 'row', axis=0, tiled=True)]
    unnamed x12 -> x45, local copies, waits for them, and re-layouts: 25.2 us -> 46.6 us
  transfers between devices with their start and end apart: 4 -> 18, of which waited for: 4 -> 18; matrix products, arithmetic and copies ran while one was open for 7% -> 9% of each run, Pallas kernels for 0% -> 0%
where the time goes in v1:
time: 585 us; the launch traced here: 584 us
  waiting for transfers between devices  413 us (71%)
  local copies, waits for them, and re-layouts  73.1 us (12%)
  starting transfers between devices  44.8 us (8%)
  other arithmetic  19.4 us (3%)
  matrix products  19.2 us (3%)
  between operations  14.2 us (2%)
    all_to_all x1, waiting for transfers between devices, shards(): lax.all_to_all(data_real, 'row', split_axis=1, concat_axis=0, tiled=True)  143 us
    ppermute x15, waiting for transfers between devices, gather_by_hops(): blocks = [lax.ppermute(blocks[0], mesh_axis, right), *blocks]  136 us
    all_to_all x1, waiting for transfers between devices, shards(): lax.all_to_all(data_imag, 'row', split_axis=1, concat_axis=0, tiled=True)  126 us
    unnamed x45, local copies, waits for them, and re-layouts  46.6 us
    all_to_all x1, starting transfers between devices, shards(): lax.all_to_all(data_imag, 'row', split_axis=1, concat_axis=0, tiled=True)  36.5 us
    convert_element_type x1, other arithmetic, shards(): sym_imag = ((forward * data_imag.astype(jnp.float32) + backward * mirror_...  18.6 us
  transfers between devices with their start and end apart: 18, of which 18 were waited for; matrix products, arithmetic and copies ran while one was open for 9% of the time, Pallas kernels for 0%

profile of v1, /device:TPU:0, one launch (start us, length us, event | category | flops | bytes accessed | tf_op | source)
XLA Modules:
  0.0 583.9 jit_solution(3168229009392243795)
XLA Ops:
  7.2 7.5 %copy.17 = bf16[64,16,8,512]{3,2,0,1:T(8,128)(2,1)} copy(bf16[64,16,8,512]{3,2,1,0:T(8,128)(2,1)} %bitcast.68) | data formatting | bytes 16777216 | tf_op jit(solution)/shard_map/all_to_all | solution.py:46
  14.7 7.4 %all-to-all-start = ((bf16[512,16,512]{2,0,1:T(8,128)(2,1)}), bf16[512,16,512]{2,0,1:T(8,128)(2,1)}, u32[]{:S(2)}, u32[]{:S(2)}) async-start(bf16[512,16,512]{2,0,1:T(8,128)(2,1)} %bitcast.71), calls=%async_computation | async-start | bytes 16777216 | tf_op jit(solution)/shard_map/all_to_all | solution.py:46
  22.1 7.6 %copy.16 = bf16[64,16,8,512]{3,2,0,1:T(8,128)(2,1)} copy(bf16[64,16,8,512]{3,2,1,0:T(8,128)(2,1)} %bitcast.69) | data formatting | bytes 16777216 | tf_op jit(solution)/shard_map/all_to_all | solution.py:47
  29.7 143.1 %all-to-all-done = bf16[512,16,512]{2,0,1:T(8,128)(2,1)} async-done(((bf16[512,16,512]{2,0,1:T(8,128)(2,1)}), bf16[512,16,512]{2,0,1:T(8,128)(2,1)}, u32[]{:S(2)}, u32[]{:S(2)}) %all-to-all-start) | async-done | bytes 8388640 | tf_op jit(solution)/shard_map/all_to_all | solution.py:46
  172.8 36.5 %all-to-all-start.1 = ((bf16[512,16,512]{2,0,1:T(8,128)(2,1)}), bf16[512,16,512]{2,0,1:T(8,128)(2,1)}, u32[]{:S(2)}, u32[]{:S(2)}) async-start(bf16[512,16,512]{2,0,1:T(8,128)(2,1)} %bitcast.70), calls=%async_computation.1 | async-start | bytes 16777216 | tf_op jit(solution)/shard_map/all_to_all | solution.py:47
  209.4 11.8 %copy.6 = bf16[512,8192]{0,1:T(8,128)(2,1)} copy(bf16[512,8192]{1,0:T(8,128)(2,1)} %param.6) | data formatting | bytes 16777216 | tf_op args[0]
  221.3 12.0 %copy.8 = bf16[512,8192]{0,1:T(8,128)(2,1)} copy(bf16[512,8192]{1,0:T(8,128)(2,1)} %param.7) | data formatting | bytes 16777216 | tf_op args[1]
  234.0 126.1 %all-to-all-done.1 = bf16[512,16,512]{2,0,1:T(8,128)(2,1)} async-done(((bf16[512,16,512]{2,0,1:T(8,128)(2,1)}), bf16[512,16,512]{2,0,1:T(8,128)(2,1)}, u32[]{:S(2)}, u32[]{:S(2)}) %all-to-all-start.1) | async-done | bytes 8388640 | tf_op jit(solution)/shard_map/all_to_all | solution.py:47
  360.1 18.6 %fusion.5 = (bf16[512,8192]{0,1:T(8,128)(2,1)}, bf16[512,8192]{0,1:T(8,128)(2,1)}) fusion(bf16[512,8192]{0,1:T(8,128)(2,1)} %copy.8, f32[512,8]{0,1:T(8,128)S(1)} %fusion.17, f32[512,8]{0,1:T(8,128)S(1)} %fusion.18, bf16[512,16,512]{2,0,1:T(8,128)(2,1)} %all-to-all-done.1, bf16[512,16,512]{2,0,1:T(8,128)(2,1)} %all-to-all-done, bf16[512,8192]{0,1:T(8,128)(2,1)} %copy.6), kind=kLoop, calls=%fused_computation.12 | loop fusion | flops 67108864 | bytes 50364416 | tf_op jit(solution)/shard_map/convert_element_type | solution.py:59
  378.6 5.3 gather_fusion
  384.0 5.3 gather_fusion.1
  389.3 0.8 select_bitcast_fusion
  390.1 0.8 collective-permute-start
  390.8 36.9 %collective-permute-done = bf16[512,128]{0,1:T(8,128)(2,1)S(1)} collective-permute-done((bf16[512,128]{0,1:T(8,128)(2,1)S(1)}, bf16[512,128]{0,1:T(8,128)(2,1)S(1)}, u32[]{:S(2)}, u32[]{:S(2)}) %collective-permute-start) | collective-permute-done | bytes 131104 | tf_op jit(solution)/shard_map/ppermute | solution.py:15
  427.7 7.1 %collective-permute-done.1 = bf16[512,128]{0,1:T(8,128)(2,1)S(1)} collective-permute-done((bf16[512,128]{0,1:T(8,128)(2,1)S(1)}, bf16[512,128]{0,1:T(8,128)(2,1)S(1)}, u32[]{:S(2)}, u32[]{:S(2)}) %collective-permute-start.1) | collective-permute-done | bytes 131104 | tf_op jit(solution)/shard_map/ppermute | solution.py:15
  434.8 7.1 %collective-permute-done.2 = bf16[512,128]{0,1:T(8,128)(2,1)S(1)} collective-permute-done((bf16[512,128]{0,1:T(8,128)(2,1)S(1)}, bf16[512,128]{0,1:T(8,128)(2,1)S(1)}, u32[]{:S(2)}, u32[]{:S(2)}) %collective-permute-start.2) | collective-permute-done | bytes 131104 | tf_op jit(solution)/shard_map/ppermute | solution.py:15
  441.9 7.1 %collective-permute-done.3 = bf16[512,128]{0,1:T(8,128)(2,1)S(1)} collective-permute-done((bf16[512,128]{0,1:T(8,128)(2,1)S(1)}, bf16[512,128]{0,1:T(8,128)(2,1)S(1)}, u32[]{:S(2)}, u32[]{:S(2)}) %collective-permute-start.3) | collective-permute-done | bytes 131104 | tf_op jit(solution)/shard_map/ppermute | solution.py:15
  449.0 7.1 %collective-permute-done.4 = bf16[512,128]{0,1:T(8,128)(2,1)S(1)} collective-permute-done((bf16[512,128]{0,1:T(8,128)(2,1)S(1)}, bf16[512,128]{0,1:T(8,128)(2,1)S(1)}, u32[]{:S(2)}, u32[]{:S(2)}) %collective-permute-start.4) | collective-permute-done | bytes 131104 | tf_op jit(solution)/shard_map/ppermute | solution.py:15
  456.1 7.1 %collective-permute-done.5 = bf16[512,128]{0,1:T(8,128)(2,1)S(1)} collective-permute-done((bf16[512,128]{0,1:T(8,128)(2,1)S(1)}, bf16[512,128]{0,1:T(8,128)(2,1)S(1)}, u32[]{:S(2)}, u32[]{:S(2)}) %collective-permute-start.5) | collective-permute-done | bytes 131104 | tf_op jit(solution)/shard_map/ppermute | solution.py:15
  463.2 7.1 %collective-permute-done.6 = bf16[512,128]{0,1:T(8,128)(2,1)S(1)} collective-permute-done((bf16[512,128]{0,1:T(8,128)(2,1)S(1)}, bf16[512,128]{0,1:T(8,128)(2,1)S(1)}, u32[]{:S(2)}, u32[]{:S(2)}) %collective-permute-start.6) | collective-permute-done | bytes 131104 | tf_op jit(solution)/shard_map/ppermute | solution.py:15
  470.3 7.1 %collective-permute-done.7 = bf16[512,128]{0,1:T(8,128)(2,1)S(1)} collective-permute-done((bf16[512,128]{0,1:T(8,128)(2,1)S(1)}, bf16[512,128]{0,1:T(8,128)(2,1)S(1)}, u32[]{:S(2)}, u32[]{:S(2)}) %collective-permute-start.7) | collective-permute-done | bytes 131104 | tf_op jit(solution)/shard_map/ppermute | solution.py:15
  477.4 7.1 %collective-permute-done.8 = bf16[512,128]{0,1:T(8,128)(2,1)S(1)} collective-permute-done((bf16[512,128]{0,1:T(8,128)(2,1)S(1)}, bf16[512,128]{0,1:T(8,128)(2,1)S(1)}, u32[]{:S(2)}, u32[]{:S(2)}) %collective-permute-start.8) | collective-permute-done | bytes 131104 | tf_op jit(solution)/shard_map/ppermute | solution.py:15
  484.5 7.1 %collective-permute-done.9 = bf16[512,128]{0,1:T(8,128)(2,1)S(1)} collective-permute-done((bf16[512,128]{0,1:T(8,128)(2,1)S(1)}, bf16[512,128]{0,1:T(8,128)(2,1)S(1)}, u32[]{:S(2)}, u32[]{:S(2)}) %collective-permute-start.9) | collective-permute-done | bytes 131104 | tf_op jit(solution)/shard_map/ppermute | solution.py:15
  491.6 7.1 %collective-permute-done.10 = bf16[512,128]{0,1:T(8,128)(2,1)S(1)} collective-permute-done((bf16[512,128]{0,1:T(8,128)(2,1)S(1)}, bf16[512,128]{0,1:T(8,128)(2,1)S(1)}, u32[]{:S(2)}, u32[]{:S(2)}) %collective-permute-start.10) | collective-permute-done | bytes 131104 | tf_op jit(solution)/shard_map/ppermute | solution.py:15
  498.6 7.1 %collective-permute-done.11 = bf16[512,128]{0,1:T(8,128)(2,1)S(1)} collective-permute-done((bf16[512,128]{0,1:T(8,128)(2,1)S(1)}, bf16[512,128]{0,1:T(8,128)(2,1)S(1)}, u32[]{:S(2)}, u32[]{:S(2)}) %collective-permute-start.11) | collective-permute-done | bytes 131104 | tf_op jit(solution)/shard_map/ppermute | solution.py:15
  505.7 7.1 %collective-permute-done.12 = bf16[512,128]{0,1:T(8,128)(2,1)S(1)} collective-permute-done((bf16[512,128]{0,1:T(8,128)(2,1)S(1)}, bf16[512,128]{0,1:T(8,128)(2,1)S(1)}, u32[]{:S(2)}, u32[]{:S(2)}) %collective-permute-start.12) | collective-permute-done | bytes 131104 | tf_op jit(solution)/shard_map/ppermute | solution.py:15
  512.9 7.1 %collective-permute-done.13 = bf16[512,128]{0,1:T(8,128)(2,1)S(1)} collective-permute-done((bf16[512,128]{0,1:T(8,128)(2,1)S(1)}, bf16[512,128]{0,1:T(8,128)(2,1)S(1)}, u32[]{:S(2)}, u32[]{:S(2)}) %collective-permute-start.13) | collective-permute-done | bytes 131104 | tf_op jit(solution)/shard_map/ppermute | solution.py:15
  519.9 7.3 %collective-permute-done.14 = bf16[512,128]{0,1:T(8,128)(2,1)S(1)} collective-permute-done((bf16[512,128]{0,1:T(8,128)(2,1)S(1)}, bf16[512,128]{0,1:T(8,128)(2,1)S(1)}, u32[]{:S(2)}, u32[]{:S(2)}) %collective-permute-start.14) | collective-permute-done | bytes 131104 | tf_op jit(solution)/shard_map/ppermute | solution.py:15
  527.9 0.7 constant_dynamic-update-slice_fusion.30
  528.6 0.7 constant_dynamic-update-slice_fusion.29
  529.9 0.7 constant_dynamic-update-slice_fusion.27
  530.6 0.7 constant_dynamic-update-slice_fusion.26
  532.0 0.7 constant_dynamic-update-slice_fusion.24
  532.7 0.7 constant_dynamic-update-slice_fusion.23
  534.7 0.7 constant_dynamic-update-slice_fusion.20
  538.1 0.7 constant_dynamic-update-slice_fusion.15
  539.4 0.7 constant_dynamic-update-slice_fusion.13
  540.1 0.7 constant_dynamic-update-slice_fusion.12
  544.2 0.7 constant_dynamic-update-slice_fusion.6
  545.5 0.7 constant_dynamic-update-slice_fusion.4
  546.2 0.7 constant_dynamic-update-slice_fusion.3
  548.9 7.6 %all-gather.2.cloned.1.call-done = bf16[8192,128]{0,1:T(8,128)(2,1)} async-done(((bf16[512,128]{0,1:T(8,128)(2,1)}), bf16[8192,128]{0,1:T(8,128)(2,1)}) %all-gather.2.cloned.1.call-update) | async-done | bytes 2097168 | tf_op jit(solution)/shard_map/all_gather | solution.py:64
  556.6 5.3 fusion.29
  561.9 5.4 fusion.14
  567.4 4.9 fusion.30
  572.3 3.0 fusion.11
  575.4 0.8 copy.10
  576.2 0.8 copy.11
  (54 shorter events, 13.7 us)
Async XLA Ops:
  14.7 158.2 %all-to-all-start = ((bf16[512,16,512]{2,0,1:T(8,128)(2,1)}), bf16[512,16,512]{2,0,1:T(8,128)(2,1)}, u32[]{:S(2)}, u32[]{:S(2)}) async-start(bf16[512,16,512]{2,0,1:T(8,128)(2,1)} %bitcast.71), calls=%async_computation | async-start | bytes 16777216 | tf_op jit(solution)/shard_map/all_to_all | solution.py:46
  172.8 187.3 %all-to-all-start.1 = ((bf16[512,16,512]{2,0,1:T(8,128)(2,1)}), bf16[512,16,512]{2,0,1:T(8,128)(2,1)}, u32[]{:S(2)}, u32[]{:S(2)}) async-start(bf16[512,16,512]{2,0,1:T(8,128)(2,1)} %bitcast.70), calls=%async_computation.1 | async-start | bytes 16777216 | tf_op jit(solution)/shard_map/all_to_all | solution.py:47
  209.4 347.2 %all-gather.2.cloned.1.call-start = ((), (), s32[]{:S(2)}) async-start(), calls=%async_computation.2 | async-start | bytes 2228224 | tf_op jit(solution)/shard_map/all_gather | solution.py:64
  221.3 12.0 %copy-start.2 = (s32[128]{0:T(128)S(1)}, s32[128]{0:T(128)}, u32[]{:S(2)}) copy-start(s32[128]{0:T(128)} %param.9) | copy-start | bytes 1540
  221.3 12.1 %copy-start.1 = (s32[8,8]{1,0:T(8,128)S(1)}, s32[8,8]{1,0:T(8,128)}, u32[]{:S(2)}) copy-start(s32[8,8]{1,0:T(8,128)} %param.8) | copy-start | bytes 772
  390.1 37.7 %collective-permute-start = (bf16[512,128]{0,1:T(8,128)(2,1)S(1)}, bf16[512,128]{0,1:T(8,128)(2,1)S(1)}, u32[]{:S(2)}, u32[]{:S(2)}) collective-permute-start(bf16[512,128]{0,1:T(8,128)(2,1)S(1)} %get-tuple-element.9), channel_id=1, source_target_pairs={{0,1},{1,2},{2,3},{3,4},{4,5},{5,6},{6,7},{7,8},{8,9},{9,10},{10,1... | collective-permute-start | bytes 393224 | tf_op jit(solution)/shard_map/ppermute | solution.py:15
  427.7 7.1 %collective-permute-start.1 = (bf16[512,128]{0,1:T(8,128)(2,1)S(1)}, bf16[512,128]{0,1:T(8,128)(2,1)S(1)}, u32[]{:S(2)}, u32[]{:S(2)}) collective-permute-start(bf16[512,128]{0,1:T(8,128)(2,1)S(1)} %collective-permute-done), channel_id=1, source_target_pairs={{0,1},{1,2},{2,3},{3,4},{4,5},{5,6},{6,7},{7,8},{8,9},{9,10},{10,1... | collective-permute-start | bytes 393224 | tf_op jit(solution)/shard_map/ppermute | solution.py:15
  434.8 7.1 %collective-permute-start.2 = (bf16[512,128]{0,1:T(8,128)(2,1)S(1)}, bf16[512,128]{0,1:T(8,128)(2,1)S(1)}, u32[]{:S(2)}, u32[]{:S(2)}) collective-permute-start(bf16[512,128]{0,1:T(8,128)(2,1)S(1)} %collective-permute-done.1), channel_id=1, source_target_pairs={{0,1},{1,2},{2,3},{3,4},{4,5},{5,6},{6,7},{7,8},{8,9},{9,10},{10,1... | collective-permute-start | bytes 393224 | tf_op jit(solution)/shard_map/ppermute | solution.py:15
  441.9 7.1 %collective-permute-start.3 = (bf16[512,128]{0,1:T(8,128)(2,1)S(1)}, bf16[512,128]{0,1:T(8,128)(2,1)S(1)}, u32[]{:S(2)}, u32[]{:S(2)}) collective-permute-start(bf16[512,128]{0,1:T(8,128)(2,1)S(1)} %collective-permute-done.2), channel_id=1, source_target_pairs={{0,1},{1,2},{2,3},{3,4},{4,5},{5,6},{6,7},{7,8},{8,9},{9,10},{10,1... | collective-permute-start | bytes 393224 | tf_op jit(solution)/shard_map/ppermute | solution.py:15
  449.0 7.1 %collective-permute-start.4 = (bf16[512,128]{0,1:T(8,128)(2,1)S(1)}, bf16[512,128]{0,1:T(8,128)(2,1)S(1)}, u32[]{:S(2)}, u32[]{:S(2)}) collective-permute-start(bf16[512,128]{0,1:T(8,128)(2,1)S(1)} %collective-permute-done.3), channel_id=1, source_target_pairs={{0,1},{1,2},{2,3},{3,4},{4,5},{5,6},{6,7},{7,8},{8,9},{9,10},{10,1... | collective-permute-start | bytes 393224 | tf_op jit(solution)/shard_map/ppermute | solution.py:15
  456.1 7.1 %collective-permute-start.5 = (bf16[512,128]{0,1:T(8,128)(2,1)S(1)}, bf16[512,128]{0,1:T(8,128)(2,1)S(1)}, u32[]{:S(2)}, u32[]{:S(2)}) collective-permute-start(bf16[512,128]{0,1:T(8,128)(2,1)S(1)} %collective-permute-done.4), channel_id=1, source_target_pairs={{0,1},{1,2},{2,3},{3,4},{4,5},{5,6},{6,7},{7,8},{8,9},{9,10},{10,1... | collective-permute-start | bytes 393224 | tf_op jit(solution)/shard_map/ppermute | solution.py:15
  463.2 7.1 %collective-permute-start.6 = (bf16[512,128]{0,1:T(8,128)(2,1)S(1)}, bf16[512,128]{0,1:T(8,128)(2,1)S(1)}, u32[]{:S(2)}, u32[]{:S(2)}) collective-permute-start(bf16[512,128]{0,1:T(8,128)(2,1)S(1)} %collective-permute-done.5), channel_id=1, source_target_pairs={{0,1},{1,2},{2,3},{3,4},{4,5},{5,6},{6,7},{7,8},{8,9},{9,10},{10,1... | collective-permute-start | bytes 393224 | tf_op jit(solution)/shard_map/ppermute | solution.py:15
  470.3 7.1 %collective-permute-start.7 = (bf16[512,128]{0,1:T(8,128)(2,1)S(1)}, bf16[512,128]{0,1:T(8,128)(2,1)S(1)}, u32[]{:S(2)}, u32[]{:S(2)}) collective-permute-start(bf16[512,128]{0,1:T(8,128)(2,1)S(1)} %collective-permute-done.6), channel_id=1, source_target_pairs={{0,1},{1,2},{2,3},{3,4},{4,5},{5,6},{6,7},{7,8},{8,9},{9,10},{10,1... | collective-permute-start | bytes 393224 | tf_op jit(solution)/shard_map/ppermute | solution.py:15
  477.4 7.1 %collective-permute-start.8 = (bf16[512,128]{0,1:T(8,128)(2,1)S(1)}, bf16[512,128]{0,1:T(8,128)(2,1)S(1)}, u32[]{:S(2)}, u32[]{:S(2)}) collective-permute-start(bf16[512,128]{0,1:T(8,128)(2,1)S(1)} %collective-permute-done.7), channel_id=1, source_target_pairs={{0,1},{1,2},{2,3},{3,4},{4,5},{5,6},{6,7},{7,8},{8,9},{9,10},{10,1... | collective-permute-start | bytes 393224 | tf_op jit(solution)/shard_map/ppermute | solution.py:15
  484.5 7.1 %collective-permute-start.9 = (bf16[512,128]{0,1:T(8,128)(2,1)S(1)}, bf16[512,128]{0,1:T(8,128)(2,1)S(1)}, u32[]{:S(2)}, u32[]{:S(2)}) collective-permute-start(bf16[512,128]{0,1:T(8,128)(2,1)S(1)} %collective-permute-done.8), channel_id=1, source_target_pairs={{0,1},{1,2},{2,3},{3,4},{4,5},{5,6},{6,7},{7,8},{8,9},{9,10},{10,1... | collective-permute-start | bytes 393224 | tf_op jit(solution)/shard_map/ppermute | solution.py:15
  491.6 7.1 %collective-permute-start.10 = (bf16[512,128]{0,1:T(8,128)(2,1)S(1)}, bf16[512,128]{0,1:T(8,128)(2,1)S(1)}, u32[]{:S(2)}, u32[]{:S(2)}) collective-permute-start(bf16[512,128]{0,1:T(8,128)(2,1)S(1)} %collective-permute-done.9), channel_id=1, source_target_pairs={{0,1},{1,2},{2,3},{3,4},{4,5},{5,6},{6,7},{7,8},{8,9},{9,10},{10,1... | collective-permute-start | bytes 393224 | tf_op jit(solution)/shard_map/ppermute | solution.py:15
  498.6 7.1 %collective-permute-start.11 = (bf16[512,128]{0,1:T(8,128)(2,1)S(1)}, bf16[512,128]{0,1:T(8,128)(2,1)S(1)}, u32[]{:S(2)}, u32[]{:S(2)}) collective-permute-start(bf16[512,128]{0,1:T(8,128)(2,1)S(1)} %collective-permute-done.10), channel_id=1, source_target_pairs={{0,1},{1,2},{2,3},{3,4},{4,5},{5,6},{6,7},{7,8},{8,9},{9,10},{10,1... | collective-permute-start | bytes 393224 | tf_op jit(solution)/shard_map/ppermute | solution.py:15
  505.7 7.1 %collective-permute-start.12 = (bf16[512,128]{0,1:T(8,128)(2,1)S(1)}, bf16[512,128]{0,1:T(8,128)(2,1)S(1)}, u32[]{:S(2)}, u32[]{:S(2)}) collective-permute-start(bf16[512,128]{0,1:T(8,128)(2,1)S(1)} %collective-permute-done.11), channel_id=1, source_target_pairs={{0,1},{1,2},{2,3},{3,4},{4,5},{5,6},{6,7},{7,8},{8,9},{9,10},{10,1... | collective-permute-start | bytes 393224 | tf_op jit(solution)/shard_map/ppermute | solution.py:15
  512.8 7.1 %collective-permute-start.13 = (bf16[512,128]{0,1:T(8,128)(2,1)S(1)}, bf16[512,128]{0,1:T(8,128)(2,1)S(1)}, u32[]{:S(2)}, u32[]{:S(2)}) collective-permute-start(bf16[512,128]{0,1:T(8,128)(2,1)S(1)} %collective-permute-done.12), channel_id=1, source_target_pairs={{0,1},{1,2},{2,3},{3,4},{4,5},{5,6},{6,7},{7,8},{8,9},{9,10},{10,1... | collective-permute-start | bytes 393224 | tf_op jit(solution)/shard_map/ppermute | solution.py:15
  519.9 7.3 %collective-permute-start.14 = (bf16[512,128]{0,1:T(8,128)(2,1)S(1)}, bf16[512,128]{0,1:T(8,128)(2,1)S(1)}, u32[]{:S(2)}, u32[]{:S(2)}) collective-permute-start(bf16[512,128]{0,1:T(8,128)(2,1)S(1)} %collective-permute-done.13), channel_id=1, source_target_pairs={{0,1},{1,2},{2,3},{3,4},{4,5},{5,6},{6,7},{7,8},{8,9},{9,10},{10,1... | collective-permute-start | bytes 393224 | tf_op jit(solution)/shard_map/ppermute | solution.py:15
  561.9 5.5 copy-start
  561.9 10.4 %slice-start = ((s8[8388608]{0:T(1024)(128)(4,1)}), s8[4194304]{0:T(1024)(128)(4,1)S(1)}, s32[]{:S(2)}) async-start(s8[8388608]{0:T(1024)(128)(4,1)} %bitcast.66), calls=%async_computation.3 | async-start | bytes 8388608
  567.3 4.9 slice-start.1
Sparse Core Ops, SparseCore 0:
  513.0 43.5 all-gather.1
